TPU v7x, 32 devices: a whole 2x2x4 slice. The times are simulated.
32 devices in a mesh: fsdp: 4 (over y, core), ctx: 2 (over x), tp: 4 (over z).
Axes of the slice: x: 2, y: 2, z: 4, core: 2. Of those that a mesh axis runs over, the one named last changes fastest.
Arguments:
- tokens: bfloat16 [4, 1024, 2048], P('fsdp', 'ctx'), may hold values from -6 to 6
- lengths: int32 [4, 3], P('fsdp'), may hold values from 1 to 768, 960 in all within a row
- block_order: int32 [4, 4], P('fsdp'), may hold values from 0 to 3, each once within a row
- ln_gain: bfloat16 [2048], P('fsdp'), may hold values from 0.25 to 1.75
- ln_bias: bfloat16 [2048], P('fsdp'), may hold values from -3 to 3
- qkv_weight: bfloat16 [2048, 3, 2048], P('fsdp', None, 'tp'), may hold values from -0.125 to 0.125
- qkv_bias: bfloat16 [3, 2048], P(None, 'tp'), may hold values from -0.59765625 to 0.59765625
- dense_weight: bfloat16 [2048, 2048], P('fsdp', 'tp'), may hold values from -1 to 1
- dense_bias: bfloat16 [2048], P('fsdp'), may hold values from -3 to 3
- fc1_weight: bfloat16 [2048, 8192], P('fsdp', 'tp'), may hold values from -0.125 to 0.125
- fc1_bias: bfloat16 [8192], P('tp'), may hold values from -3 to 3
- fc2_weight: bfloat16 [2048, 8192], P('fsdp', 'tp'), may hold values from -0.0625 to 0.0625
- fc2_bias: bfloat16 [2048], P('fsdp'), may hold values from -3 to 3
- cotangent: bfloat16 [4, 1024, 2048], P('fsdp', 'ctx'), may hold values from -6 to 6
Outputs:
- output: bfloat16 [4, 1024, 2048], P('fsdp', 'ctx')
- input_grad: float32 [4, 1024, 2048], P('fsdp', 'ctx')
- ln_gain_grad: float32 [2048], P('fsdp')
- ln_bias_grad: float32 [2048], P('fsdp')
- qkv_weight_grad: float32 [2048, 3, 2048], P('fsdp', None, 'tp')
- qkv_bias_grad: float32 [3, 2048], P(None, 'tp')
- dense_weight_grad: float32 [2048, 2048], P('fsdp', 'tp')
- dense_bias_grad: float32 [2048], P('fsdp')
- fc1_weight_grad: float32 [2048, 8192], P('fsdp', 'tp')
- fc1_bias_grad: float32 [8192], P('tp')
- fc2_weight_grad: float32 [2048, 8192], P('fsdp', 'tp')
- fc2_bias_grad: float32 [2048], P('fsdp')
Inputs may be any that keep to these rules, and one draw needn't show every extreme that they name: Each row holds the lengths of 3 sequences packed from the row's start; they sum to 960 and the largest is exactly 768. Each row is a permutation of the 4 block numbers; dealt block j holds packed block block_order[b, j].
All inputs are finite; a program needn't handle non-finite values.
Results may differ from a plain program's by a relative error of at most 0.012.
Values may be sent and summed in bfloat16 or wider, within the bound.
No kernel may reach another device: no remote copies, remote signals or barrier semaphores. Data moves between devices by JAX's collectives and lax.ppermute only.
A program may use at most 256 MiB of HBM per device.

v0:
```python
import math
import jax
import jax.numpy as jnp
from jax import lax
from jax.sharding import PartitionSpec as P

HD = 256
ROT = 64
NORM_EPSILON = 1e-05
MASK_FLOOR = -1000000000.0


def rotation_tables(position):
    frequency = jnp.exp(jnp.arange(ROT // 2, dtype=jnp.float32) * (-2.0 * math.log(10000.0) / ROT))
    angles = position.astype(jnp.float32)[:, None] * frequency[None, :]
    return (jnp.cos(angles)[:, None, :], jnp.sin(angles)[:, None, :])


def rotate(values, cosine_table, sine_table):
    first_half = values[..., : ROT // 2]
    second_half = values[..., ROT // 2 : ROT]
    return jnp.concatenate(
        [
            first_half * cosine_table - second_half * sine_table,
            second_half * cosine_table + first_half * sine_table,
            values[..., ROT:],
        ],
        axis=-1,
    )


def rotate_back(grads, cosine_table, sine_table):
    first_half = grads[..., : ROT // 2]
    second_half = grads[..., ROT // 2 : ROT]
    return jnp.concatenate(
        [
            first_half * cosine_table + second_half * sine_table,
            second_half * cosine_table - first_half * sine_table,
            grads[..., ROT:],
        ],
        axis=-1,
    )


def packed_rows(order_row, first_slot, row_count, block_rows):
    row_index = jnp.arange(row_count, dtype=jnp.int32)
    dealt_slot = first_slot + row_index // block_rows
    selector = dealt_slot[:, None] == jnp.arange(order_row.shape[0], dtype=jnp.int32)[None, :]
    source_block = jnp.sum(jnp.where(selector, order_row[None, :], 0), axis=1, dtype=jnp.int32)
    return source_block * block_rows + row_index % block_rows


def place_rows(packed_at, lengths_row):
    seq_ends = jnp.cumsum(lengths_row, dtype=jnp.int32)
    passed = packed_at[:, None] >= seq_ends[None, :]
    segment = jnp.sum(passed.astype(jnp.int32), axis=1, dtype=jnp.int32)
    before = jnp.sum(jnp.where(passed, lengths_row[None, :], 0), axis=1, dtype=jnp.int32)
    return (segment, packed_at - before)


def gelu_slope(value):
    normal_cdf = 0.5 * (1.0 + lax.erf(value * (1.0 / math.sqrt(2.0))))
    density = jnp.exp(-0.5 * value * value) * (1.0 / math.sqrt(2.0 * math.pi))
    return normal_cdf + value * density


def per_device(
    tokens,
    lengths,
    block_order,
    ln_gain,
    ln_bias,
    qkv_weight,
    qkv_bias,
    dense_weight,
    dense_bias,
    fc1_weight,
    fc1_bias,
    fc2_weight,
    fc2_bias,
    cotangent,
):
    gathered = (
        lax.all_gather(qkv_weight, "fsdp", axis=0, tiled=True),
        lax.all_gather(dense_weight, "fsdp", axis=0, tiled=True),
        lax.all_gather(fc1_weight, "fsdp", axis=0, tiled=True),
        lax.all_gather(fc2_weight, "fsdp", axis=0, tiled=True),
        lax.all_gather(ln_gain, "fsdp", axis=0, tiled=True),
        lax.all_gather(ln_bias, "fsdp", axis=0, tiled=True),
        lax.all_gather(dense_bias, "fsdp", axis=0, tiled=True),
        lax.all_gather(fc2_bias, "fsdp", axis=0, tiled=True),
    )
    qkv_full = gathered[0]
    dense_full = gathered[1]
    fc1_full = gathered[2]
    fc2_full = gathered[3]
    norm_gain = gathered[4].astype(jnp.float32)
    norm_bias = gathered[5].astype(jnp.float32)
    out_bias = gathered[6].astype(jnp.float32) + gathered[7].astype(jnp.float32)
    inputs = tokens[0].astype(jnp.float32)
    row_count = inputs.shape[0]
    block_rows = row_count // 2
    group_rows = row_count * lax.axis_size("ctx")
    lengths_row = lengths[0]
    order_row = block_order[0]
    seq_count = lengths_row.shape[0]
    local_packed = packed_rows(order_row, lax.axis_index("ctx") * 2, row_count, block_rows)
    key_packed = packed_rows(order_row, 0, group_rows, block_rows)
    local_segment, local_position = place_rows(local_packed, lengths_row)
    key_segment = place_rows(key_packed, lengths_row)[0]
    valid_rows = (local_segment < seq_count).astype(jnp.float32)
    allowed = (local_segment[:, None] == key_segment[None, :]) & (
        key_packed[None, :] <= local_packed[:, None]
    )
    cosine_table, sine_table = rotation_tables(local_position)
    score_scale = 1.0 / math.sqrt(HD)
    row_mean = jnp.mean(inputs, axis=1, keepdims=True)
    centred = inputs - row_mean
    variance = jnp.mean(centred * centred, axis=1, keepdims=True)
    inverse = lax.rsqrt(variance + NORM_EPSILON)
    standard = centred * inverse
    normed = (standard * norm_gain + norm_bias).astype(jnp.bfloat16)
    projected = jnp.einsum(
        "td,dce->tce", normed, qkv_full, preferred_element_type=jnp.float32
    ) + qkv_bias.astype(jnp.float32)
    heads_here = projected.shape[2] // HD
    shaped = projected.reshape(row_count, 3, heads_here, HD)
    queries = rotate(shaped[:, 0], cosine_table, sine_table).astype(jnp.bfloat16)
    keys_local = rotate(shaped[:, 1], cosine_table, sine_table).astype(jnp.bfloat16)
    values_local = shaped[:, 2].astype(jnp.bfloat16)
    keys_all, values_all = (
        lax.all_gather(keys_local, "ctx", axis=0, tiled=True),
        lax.all_gather(values_local, "ctx", axis=0, tiled=True),
    )

    def head_scores(head_index):
        scores = (
            jnp.einsum(
                "qe,ke->qk",
                queries[:, head_index],
                keys_all[:, head_index],
                preferred_element_type=jnp.float32,
            )
            * score_scale
        )
        return jnp.where(allowed, scores, MASK_FLOOR)

    head_outputs = []
    log_totals = []
    for head_index in range(heads_here):
        scores = head_scores(head_index)
        row_max = jnp.max(scores, axis=1, keepdims=True)
        exp_scores = jnp.exp(scores - row_max)
        row_total = jnp.sum(exp_scores, axis=1, keepdims=True)
        probabilities = (exp_scores / row_total).astype(jnp.bfloat16)
        head_outputs.append(
            jnp.dot(probabilities, values_all[:, head_index], preferred_element_type=jnp.float32)
        )
        log_totals.append(row_max + jnp.log(row_total))
    attended = (
        (jnp.stack(head_outputs, axis=1) * valid_rows[:, None, None])
        .astype(jnp.bfloat16)
        .reshape(row_count, heads_here * HD)
    )
    pre_act = jnp.dot(normed, fc1_full, preferred_element_type=jnp.float32) + fc1_bias.astype(
        jnp.float32
    )
    hidden = jax.nn.gelu(pre_act, approximate=False).astype(jnp.bfloat16)
    partial_out = jnp.einsum(
        "te,de->td", attended, dense_full, preferred_element_type=jnp.float32
    ) + jnp.einsum("tf,df->td", hidden, fc2_full, preferred_element_type=jnp.float32)
    summed = lax.psum(partial_out, "tp")
    output = (inputs + summed + out_bias).astype(jnp.bfloat16)
    upstream_low = cotangent[0]
    upstream = upstream_low.astype(jnp.float32)
    out_bias_grad = jnp.sum(upstream, axis=0)
    dense_grad = jnp.einsum("td,te->de", upstream_low, attended, preferred_element_type=jnp.float32)
    fc2_grad = jnp.einsum("td,tf->df", upstream_low, hidden, preferred_element_type=jnp.float32)
    attended_grad = (
        jnp.dot(upstream_low, dense_full, preferred_element_type=jnp.float32).astype(jnp.bfloat16)
        * valid_rows[:, None].astype(jnp.bfloat16)
    ).reshape(row_count, heads_here, HD)
    hidden_grad = jnp.dot(upstream_low, fc2_full, preferred_element_type=jnp.float32)
    pre_grad = (hidden_grad * gelu_slope(pre_act)).astype(jnp.bfloat16)
    fc1_bias_grad = jnp.sum(pre_grad.astype(jnp.float32), axis=0)
    fc1_grad = jnp.einsum("td,tf->df", normed, pre_grad, preferred_element_type=jnp.float32)
    normed_grad = jnp.einsum("tf,df->td", pre_grad, fc1_full, preferred_element_type=jnp.float32)
    query_pieces = []
    key_pieces = []
    value_pieces = []
    for head_index in range(heads_here):
        probs_full = jnp.exp(head_scores(head_index) - log_totals[head_index])
        probs_low = probs_full.astype(jnp.bfloat16)
        head_grad = attended_grad[:, head_index]
        prob_grad = jnp.einsum(
            "qe,ke->qk", head_grad, values_all[:, head_index], preferred_element_type=jnp.float32
        )
        row_delta = jnp.sum(probs_full * prob_grad, axis=1, keepdims=True)
        score_grad = (probs_full * (prob_grad - row_delta)).astype(jnp.bfloat16)
        query_pieces.append(
            jnp.dot(score_grad, keys_all[:, head_index], preferred_element_type=jnp.float32)
            * score_scale
        )
        key_pieces.append(
            jnp.einsum(
                "qk,qe->ke", score_grad, queries[:, head_index], preferred_element_type=jnp.float32
            )
            * score_scale
        )
        value_pieces.append(
            jnp.einsum("qk,qe->ke", probs_low, head_grad, preferred_element_type=jnp.float32)
        )
    own_keys, own_values = (
        lax.psum_scatter(jnp.stack(key_pieces, axis=1), "ctx", scatter_dimension=0, tiled=True),
        lax.psum_scatter(jnp.stack(value_pieces, axis=1), "ctx", scatter_dimension=0, tiled=True),
    )
    query_turned = rotate_back(jnp.stack(query_pieces, axis=1), cosine_table, sine_table)
    key_turned = rotate_back(own_keys, cosine_table, sine_table)
    proj_grad = (
        jnp.stack([query_turned, key_turned, own_values], axis=1)
        .astype(jnp.bfloat16)
        .reshape(row_count, 3, heads_here * HD)
    )
    qkv_bias_grad = jnp.sum(proj_grad.astype(jnp.float32), axis=0)
    qkv_grad = jnp.einsum("td,tce->dce", normed, proj_grad, preferred_element_type=jnp.float32)
    normed_grad = normed_grad + jnp.einsum(
        "tce,dce->td", proj_grad, qkv_full, preferred_element_type=jnp.float32
    )
    full_grad = lax.psum(normed_grad, "tp")
    gain_grad = jnp.sum(full_grad * standard, axis=0)
    shift_grad = jnp.sum(full_grad, axis=0)
    scaled = full_grad * norm_gain
    input_grad = upstream + inverse * (
        scaled
        - jnp.mean(scaled, axis=1, keepdims=True)
        - standard * jnp.mean(scaled * standard, axis=1, keepdims=True)
    )
    bias_sums = lax.psum((qkv_bias_grad, fc1_bias_grad), ("fsdp", "ctx"))
    reduced = (
        lax.psum_scatter(qkv_grad, ("fsdp", "ctx"), scatter_dimension=0, tiled=True),
        lax.psum_scatter(dense_grad, ("fsdp", "ctx"), scatter_dimension=0, tiled=True),
        lax.psum_scatter(fc1_grad, ("fsdp", "ctx"), scatter_dimension=0, tiled=True),
        lax.psum_scatter(fc2_grad, ("fsdp", "ctx"), scatter_dimension=0, tiled=True),
        lax.psum_scatter(gain_grad, ("fsdp", "ctx"), scatter_dimension=0, tiled=True),
        lax.psum_scatter(shift_grad, ("fsdp", "ctx"), scatter_dimension=0, tiled=True),
        lax.psum_scatter(out_bias_grad, ("fsdp", "ctx"), scatter_dimension=0, tiled=True),
    )
    shards = (
        lax.all_gather(reduced[0], "ctx", axis=0, tiled=True),
        lax.all_gather(reduced[1], "ctx", axis=0, tiled=True),
        lax.all_gather(reduced[2], "ctx", axis=0, tiled=True),
        lax.all_gather(reduced[3], "ctx", axis=0, tiled=True),
        lax.all_gather(reduced[4], "ctx", axis=0, tiled=True),
        lax.all_gather(reduced[5], "ctx", axis=0, tiled=True),
        lax.all_gather(reduced[6], "ctx", axis=0, tiled=True),
    )
    return (
        output[None],
        input_grad[None],
        shards[4],
        shards[5],
        shards[0],
        bias_sums[0],
        shards[1],
        shards[6],
        shards[2],
        bias_sums[1],
        shards[3],
        shards[6],
    )


def solution(mesh):
    placed = (
        P("fsdp", "ctx", None),
        P("fsdp", None),
        P("fsdp", None),
        P("fsdp"),
        P("fsdp"),
        P("fsdp", None, "tp"),
        P(None, "tp"),
        P("fsdp", "tp"),
        P("fsdp"),
        P("fsdp", "tp"),
        P("tp"),
        P("fsdp", "tp"),
        P("fsdp"),
        P("fsdp", "ctx", None),
    )
    return jax.shard_map(
        per_device,
        mesh=mesh,
        in_specs=placed,
        out_specs=(
            P("fsdp", "ctx", None),
            P("fsdp", "ctx", None),
            P("fsdp"),
            P("fsdp"),
            P("fsdp", None, "tp"),
            P(None, "tp"),
            P("fsdp", "tp"),
            P("fsdp"),
            P("fsdp", "tp"),
            P("tp"),
            P("fsdp", "tp"),
            P("fsdp"),
        ),
        check_vma=False,
    )
```

profile of v0, /device:TPU:0, one launch (start us, length us, event | category | flops | bytes accessed | tf_op | source)
XLA Modules:
  0.0 1210.0 jit_solution(16124537954326559841)
XLA Ops:
  24.5 34.9 %all-gather.19.cloned.1.call-done = bf16[2048,3,512]{0,2,1:T(8,128)(2,1)} async-done(((bf16[512,3,512]{0,2,1:T(8,128)(2,1)}), bf16[2048,3,512]{0,2,1:T(8,128)(2,1)}) %all-gather.19.cloned.1.call-update) | async-done | bytes 6291472 | tf_op jit(solution)/shard_map/all_gather | solution.py:84
  69.2 14.3 %all-gather.23.cloned.1.call-done = bf16[2048,512]{1,0:T(8,128)(2,1)} async-done(((bf16[512,512]{1,0:T(8,128)(2,1)}), bf16[2048,512]{1,0:T(8,128)(2,1)}) %all-gather.23.cloned.1.call-update) | async-done | bytes 2097168 | tf_op jit(solution)/shard_map/all_gather | solution.py:85
  90.9 16.0 %all-gather.21.cloned.1.call-done = bf16[1024,2,256]{0,2,1:T(8,128)(2,1)} async-done(((bf16[512,2,256]{0,2,1:T(8,128)(2,1)}), bf16[1024,2,256]{0,2,1:T(8,128)(2,1)}) %all-gather.21.cloned.1.call-update) | async-done | bytes 1048592 | tf_op jit(solution)/shard_map/all_gather | solution.py:132
  114.5 15.7 %all-gather.37.cloned.1.call-done = bf16[1024,1,2,256]{0,3,2,1:T(8,128)(2,1)} async-done(((bf16[512,1,2,256]{0,3,2,1:T(8,128)(2,1)}), bf16[1024,1,2,256]{0,3,2,1:T(8,128)(2,1)}) %all-gather.37.cloned.1.call-update) | async-done | bytes 1048592 | tf_op jit(solution)/shard_map/all_gather | solution.py:133
  152.3 12.5 %reduce-scatter.9.cloned.1.call-done = f32[512,2,256]{2,0,1:T(8,128)} async-done(((f32[1024,2,256]{2,0,1:T(8,128)}), f32[512,2,256]{2,0,1:T(8,128)}) %reduce-scatter.9.cloned.1.call-update) | async-done | bytes 1048592 | tf_op jit(solution)/shard_map/reduce_scatter | solution.py:215
  171.0 28.4 %reduce-scatter.7.cloned.1.call-done = f32[512,2,256]{0,2,1:T(8,128)} async-done(((f32[1024,2,256]{0,2,1:T(8,128)}), f32[512,2,256]{0,2,1:T(8,128)}) %reduce-scatter.7.cloned.1.call-update) | async-done | bytes 1048592 | tf_op jit(solution)/shard_map/reduce_scatter | solution.py:214
  207.2 8.8 fusion.40
  216.7 42.6 %all-gather.25.cloned.1.call-done = bf16[2048,2048]{1,0:T(8,128)(2,1)} async-done(((bf16[512,2048]{1,0:T(8,128)(2,1)}), bf16[2048,2048]{1,0:T(8,128)(2,1)}) %all-gather.25.cloned.1.call-update) | async-done | bytes 8388624 | tf_op jit(solution)/shard_map/all_gather | solution.py:86
  259.3 17.2 %fusion.20 = (bf16[512,2048]{1,0:T(8,128)(2,1)}, f32[512,2048]{1,0:T(8,128)}) fusion(f32[2048]{0:T(1024)S(1)} %convert_element_type.135, bf16[2048,2048]{1,0:T(8,128)(2,1)} %all-gather.25.cloned.1.call-done, bf16[1,512,2048]{2,1,0:T(8,128)(2,1)S(1)} %copy-done, f32[2048]{0:T(1024)S(1)} %bitcast.223, f32[2048]{0:T(1024)S(1)} %bitcast.214, ...), kind=kOutput, calls=%fused_computation.27 | convolution fusion | flops 4370464768 | bytes 16805888 | tf_op jit(solution)/shard_map/dot_general | solution.py:165
  276.5 42.7 %all-gather.27.cloned.1.call-done = bf16[2048,2048]{1,0:T(8,128)(2,1)} async-done(((bf16[512,2048]{1,0:T(8,128)(2,1)}), bf16[2048,2048]{1,0:T(8,128)(2,1)}) %all-gather.27.cloned.1.call-update) | async-done | bytes 8388624 | tf_op jit(solution)/shard_map/all_gather | solution.py:87
  319.2 9.4 convert_reduce_fusion.2
  329.9 8.8 fusion.92
  339.2 12.5 %convolution_bitcast_fusion = f32[2048,2048]{0,1:T(8,128)} fusion(bf16[512,2048]{1,0:T(8,128)(2,1)} %get-tuple-element.96, bf16[1,512,2048]{2,1,0:T(8,128)(2,1)} %param.27), kind=kOutput, calls=%fused_computation | convolution fusion | flops 4294967296 | bytes 20971520 | tf_op jit(solution)/shard_map/td,tf->df/dot_general | solution.py:178
  353.3 10.8 fusion.99
  364.1 9.8 fusion.100
  381.0 8.7 bitcast_add_fusion
  389.8 79.9 %reduce-scatter.11.cloned.1.call-done = f32[256,3,512]{2,0,1:T(8,128)} async-done(((f32[2048,3,512]{2,0,1:T(8,128)}), f32[256,3,512]{2,0,1:T(8,128)}) %reduce-scatter.11.cloned.1.call-update) | async-done | bytes 1572880 | tf_op jit(solution)/shard_map/reduce_scatter | solution.py:240
  469.7 119.7 %reduce-scatter.15.cloned.1.call-done = f32[256,2048]{1,0:T(8,128)} async-done(((f32[2048,2048]{1,0:T(8,128)}), f32[256,2048]{1,0:T(8,128)}) %reduce-scatter.15.cloned.1.call-update) | async-done | bytes 2097168 | tf_op jit(solution)/shard_map/reduce_scatter | solution.py:242
  589.5 119.4 %reduce-scatter.17.cloned.1.call-done = f32[256,2048]{0,1:T(8,128)} async-done(((f32[2048,2048]{0,1:T(8,128)}), f32[256,2048]{0,1:T(8,128)}) %reduce-scatter.17.cloned.1.call-update) | async-done | bytes 2097168 | tf_op jit(solution)/shard_map/reduce_scatter | solution.py:243
  721.9 9.8 all-gather.31.cloned.1.call-done
  734.3 291.4 %all-reduce.7.cloned.1.call-done = (f32[512,2048]{1,0:T(8,128)}, f32[512,2048]{1,0:T(8,128)}) async-done(((f32[512,2048]{1,0:T(8,128)}, f32[512,2048]{1,0:T(8,128)}), (f32[512,2048]{1,0:T(8,128)}, f32[512,2048]{1,0:T(8,128)})) %all-reduce.7.cloned.1.call-update) | async-done | bytes 8388624 | tf_op jit(solution)/shard_map/psum | solution.py:172
  1035.8 28.5 %all-reduce.3 = (f32[2048]{0:T(1024)S(1)}, f32[2048]{0:T(1024)S(1)}, f32[3,512]{1,0:T(4,128)}, f32[2048]{0:T(1024)S(1)}, f32[2048]{0:T(1024)}) all-reduce(f32[2048]{0:T(1024)S(1)} %get-tuple-element.60, f32[2048]{0:T(1024)S(1)} %get-tuple-element.63, ...), channel_id=5, replica_groups=mesh['fsdp'=4,'ctx'=2,'tp'=4] {'fsdp','ctx'}, use_global_device_ids=true, to_apply=%region_21.22.clone | all-reduce | flops 9728 | bytes 77824
  1077.5 54.2 %all-gather.33.cloned.1.call-done = f32[512,2048]{1,0:T(8,128)} async-done(((f32[256,2048]{1,0:T(8,128)}), f32[512,2048]{1,0:T(8,128)}) %all-gather.33.cloned.1.call-update) | async-done | bytes 4194320 | tf_op jit(solution)/shard_map/all_gather | solution.py:251
  1131.6 58.1 %all-gather.35.cloned.1.call-done = f32[512,2048]{0,1:T(8,128)} async-done(((f32[256,2048]{0,1:T(8,128)}), f32[512,2048]{0,1:T(8,128)}) %all-gather.35.cloned.1.call-update) | async-done | bytes 4194320 | tf_op jit(solution)/shard_map/all_gather | solution.py:252
  (215 shorter events, 140.4 us)
Async XLA Ops:
  7.2 52.1 %all-gather.19.cloned.1.call-start = ((), (), s32[]{:S(2)}) async-start(), calls=%async_computation.6 | async-start | bytes 7864320 | tf_op jit(solution)/shard_map/all_gather | solution.py:84
  10.0 73.5 %all-gather.23.cloned.1.call-start = ((), (), s32[]{:S(2)}) async-start(), calls=%async_computation.8 | async-start | bytes 2621440 | tf_op jit(solution)/shard_map/all_gather | solution.py:85
  10.8 96.1 %all-gather.21.cloned.1.call-start = ((), (), s32[]{:S(2)}) async-start(), calls=%async_computation.7 | async-start | bytes 1572864 | tf_op jit(solution)/shard_map/all_gather | solution.py:132
  17.2 48.0 %copy-start.28 = (f32[4,1,512]{2,1,0:T(1,128)}, f32[4,1,512]{2,1,0:T(1,128)S(1)}, u32[]{:S(2)}) copy-start(f32[4,1,512]{2,1,0:T(1,128)S(1)} %convert_element_type.153) | copy-start | bytes 24580
  23.0 45.6 %copy-start.27 = (s32[512]{0:T(512)}, s32[512]{0:T(512)S(1)}, u32[]{:S(2)}) copy-start(s32[512]{0:T(512)S(1)} %get-tuple-element.65) | copy-start | bytes 6148
  24.5 41.1 %copy-start.21 = (f32[512,32]{0,1:T(8,128)}, f32[512,32]{0,1:T(8,128)S(1)}, u32[]{:S(2)}) copy-start(f32[512,32]{0,1:T(8,128)S(1)} %get-tuple-element.92) | copy-start | bytes 196612
  67.8 62.4 %all-gather.37.cloned.1.call-start = ((), (), s32[]{:S(2)}) async-start(), calls=%async_computation.21 | async-start | bytes 1572864 | tf_op jit(solution)/shard_map/all_gather | solution.py:133
  90.0 74.9 %reduce-scatter.9.cloned.1.call-start = ((), (), s32[]{:S(2)}) async-start(), calls=%async_computation.12 | async-start | bytes 3145728 | tf_op jit(solution)/shard_map/reduce_scatter | solution.py:215
  114.3 85.2 %reduce-scatter.7.cloned.1.call-start = ((), (), s32[]{:S(2)}) async-start(), calls=%async_computation.11 | async-start | bytes 3145728 | tf_op jit(solution)/shard_map/reduce_scatter | solution.py:214
  138.6 120.8 %all-gather.25.cloned.1.call-start = ((), (), s32[]{:S(2)}) async-start(), calls=%async_computation.9 | async-start | bytes 10485760 | tf_op jit(solution)/shard_map/all_gather | solution.py:86
  139.3 179.9 %all-gather.27.cloned.1.call-start = ((), (), s32[]{:S(2)}) async-start(), calls=%async_computation.10 | async-start | bytes 10485760 | tf_op jit(solution)/shard_map/all_gather | solution.py:87
  140.1 234.2 %reduce-scatter.13.cloned.1.call-start = ((), (), s32[]{:S(2)}) async-start(), calls=%async_computation.15 | async-start | bytes 4718592 | tf_op jit(solution)/shard_map/reduce_scatter | solution.py:241
  147.5 322.2 %reduce-scatter.11.cloned.1.call-start = ((), (), s32[]{:S(2)}) async-start(), calls=%async_computation.13 | async-start | bytes 14155776 | tf_op jit(solution)/shard_map/reduce_scatter | solution.py:240
  216.0 43.3 %copy-start.29 = (f32[4,1,512]{2,1,0:T(1,128)S(1)}, f32[4,1,512]{2,1,0:T(1,128)}, u32[]{:S(2)}) copy-start(f32[4,1,512]{2,1,0:T(1,128)} %copy-done.28) | copy-start | bytes 24580
  216.0 373.4 %reduce-scatter.15.cloned.1.call-start = ((), (), s32[]{:S(2)}) async-start(), calls=%async_computation.17 | async-start | bytes 18874368 | tf_op jit(solution)/shard_map/reduce_scatter | solution.py:242
  338.7 370.2 %reduce-scatter.17.cloned.1.call-start = ((), (), s32[]{:S(2)}) async-start(), calls=%async_computation.19 | async-start | bytes 18874368 | tf_op jit(solution)/shard_map/reduce_scatter | solution.py:243
  351.8 380.0 %all-gather.31.cloned.1.call-start = ((), (), s32[]{:S(2)}) async-start(), calls=%async_computation.16 | async-start | bytes 1572864 | tf_op jit(solution)/shard_map/all_gather | solution.py:250
  374.3 651.4 %all-reduce.7.cloned.1.call-start = ((), (), s32[]{:S(2)}) async-start(), calls=%async_computation.22 | async-start | bytes 16777216 | tf_op jit(solution)/shard_map/psum | solution.py:172
  389.7 319.2 %copy-start.35 = (bf16[512]{0:T(512)(128)(2,1)S(1)}, bf16[512]{0:T(512)(128)(2,1)}, u32[]{:S(2)}) copy-start(bf16[512]{0:T(512)(128)(2,1)} %param.22) | copy-start | bytes 3076
  389.8 319.2 %copy-start.36 = (bf16[512]{0:T(512)(128)(2,1)S(1)}, bf16[512]{0:T(512)(128)(2,1)}, u32[]{:S(2)}) copy-start(bf16[512]{0:T(512)(128)(2,1)} %param.26) | copy-start | bytes 3076
  389.8 319.2 %copy-start.39 = (u32[32]{0:T(128)S(1)}, u32[32]{0:T(128)}, u32[]{:S(2)}) copy-start(u32[32]{0:T(128)} %constant.160) | copy-start | bytes 388
  389.8 687.7 %all-gather.29.cloned.1.call-start = ((), (), s32[]{:S(2)}) async-start(), calls=%async_computation.14 | async-start | bytes 4718592 | tf_op jit(solution)/shard_map/all_gather | solution.py:249
  469.7 661.9 %all-gather.33.cloned.1.call-start = ((), (), s32[]{:S(2)}) async-start(), calls=%async_computation.18 | async-start | bytes 6291456 | tf_op jit(solution)/shard_map/all_gather | solution.py:251
  589.5 600.3 %all-gather.35.cloned.1.call-start = ((), (), s32[]{:S(2)}) async-start(), calls=%async_computation.20 | async-start | bytes 6291456 | tf_op jit(solution)/shard_map/all_gather | solution.py:252
  (36 other events, 216.2 us)
Sparse Core Ops, SparseCore 0:
  10.2 49.1 all-gather.18
  60.9 22.5 all-gather.22
  85.6 21.2 all-gather.20
  108.9 21.2 all-gather.36
  132.9 31.9 reduce-scatter.8
  167.5 31.8 reduce-scatter.6
  201.0 58.2 all-gather.24
  260.9 58.2 all-gather.26
  323.1 51.0 reduce-scatter.12
  377.6 92.0 reduce-scatter.10
  473.2 116.1 reduce-scatter.14
  592.9 115.9 reduce-scatter.16
  710.4 21.2 all-gather.30
  734.8 290.8 all-reduce.6
  1027.0 46.3 all-gather.28
  1074.9 56.7 all-gather.32
  1133.0 56.7 all-gather.34
where the time goes:
time: 1220 us; the launch traced here: 1210 us
  waiting for transfers between devices  942 us (77%)
  matrix products  122 us (10%)
  blocking collectives  63.4 us (5%)
  local copies, waits for them, and re-layouts  37.8 us (3%)
  other arithmetic  27.6 us (2%)
  between operations  15.6 us (1%)
    psum x1, waiting for transfers between devices, per_device(): summed = lax.psum(partial_out, 'tp')  291 us
    reduce_scatter x1, waiting for transfers between devices, per_device(): lax.psum_scatter(fc1_grad, ('fsdp', 'ctx'), scatter_dimension=0, tiled=True)  120 us
    reduce_scatter x1, waiting for transfers between devices, per_device(): lax.psum_scatter(fc2_grad, ('fsdp', 'ctx'), scatter_dimension=0, tiled=True)  119 us
    reduce_scatter x1, waiting for transfers between devices, per_device(): lax.psum_scatter(qkv_grad, ('fsdp', 'ctx'), scatter_dimension=0, tiled=True)  79.9 us
    all_gather x1, waiting for transfers between devices, per_device(): lax.all_gather(reduced[3], 'ctx', axis=0, tiled=True)  58.1 us
    all_gather x1, waiting for transfers between devices, per_device(): lax.all_gather(reduced[2], 'ctx', axis=0, tiled=True)  54.2 us
    all_gather x1, waiting for transfers between devices, per_device(): lax.all_gather(fc2_weight, 'fsdp', axis=0, tiled=True)  42.7 us
    all_gather x1, waiting for transfers between devices, per_device(): lax.all_gather(fc1_weight, 'fsdp', axis=0, tiled=True)  42.6 us
  transfers between devices with their start and end apart: 17, of which 16 were waited for; matrix products, arithmetic and copies ran while one was open for 14% of the time, Pallas kernels for 0%

commit v1 on v0

--- a/solution.py
+++ b/solution.py
@@ -8,6 +8,18 @@
 ROT = 64
 NORM_EPSILON = 1e-05
 MASK_FLOOR = -1000000000.0
+
+
+def collect(x, axis, dim):
+    ways, here, lap = (lax.axis_size(axis), lax.axis_index(axis), x.shape[dim])
+    line, have = (x, 1)
+    while have < ways:
+        line = jnp.concatenate(
+            [line, lax.ppermute(line, axis, [(d, (d - have) % ways) for d in range(ways)])],
+            axis=dim,
+        )
+        have = 2 * have
+    return jnp.roll(line, here * lap, axis=dim)
 
 
 def rotation_tables(position):
@@ -248,7 +260,7 @@
     shards = (
         lax.all_gather(reduced[0], "ctx", axis=0, tiled=True),
         lax.all_gather(reduced[1], "ctx", axis=0, tiled=True),
-        lax.all_gather(reduced[2], "ctx", axis=0, tiled=True),
+        collect(reduced[2], "ctx", 0),
         lax.all_gather(reduced[3], "ctx", axis=0, tiled=True),
         lax.all_gather(reduced[4], "ctx", axis=0, tiled=True),
         lax.all_gather(reduced[5], "ctx", axis=0, tiled=True),

time: 1220 us -> 1170 us (0.959)
  waiting for transfers between devices: 942 us -> 891 us
    all_gather x1 -> x0, waiting for transfers between devices: 54.2 us -> none  [per_device(): lax.all_gather(reduced[2], 'ctx', axis=0, tiled=True)]
    reduce_scatter x1, waiting for transfers between devices: 0.33 us -> 13.7 us  [per_device(): lax.psum_scatter(dense_grad, ('fsdp', 'ctx'), scatter_dimension=0, tiled=...]
    unnamed x103 -> x104, local copies, waits for them, and re-layouts: 26 us -> 25.3 us
  transfers between devices with their start and end apart: 17 -> 17, of which waited for: 16 -> 15; matrix products, arithmetic and copies ran while one was open for 14% -> 14% of each run, Pallas kernels for 0% -> 0%
where the time goes in v1:
time: 1170 us; the launch traced here: 1160 us
  waiting for transfers between devices  891 us (76%)
  matrix products  117 us (10%)
  blocking collectives  63.4 us (5%)
  local copies, waits for them, and re-layouts  37 us (3%)
  other arithmetic  34.3 us (3%)
  between operations  15.5 us (1%)
    psum x1, waiting for transfers between devices, per_device(): summed = lax.psum(partial_out, 'tp')  291 us
    reduce_scatter x1, waiting for transfers between devices, per_device(): lax.psum_scatter(fc1_grad, ('fsdp', 'ctx'), scatter_dimension=0, tiled=True)  120 us
    reduce_scatter x1, waiting for transfers between devices, per_device(): lax.psum_scatter(fc2_grad, ('fsdp', 'ctx'), scatter_dimension=0, tiled=True)  120 us
    reduce_scatter x1, waiting for transfers between devices, per_device(): lax.psum_scatter(qkv_grad, ('fsdp', 'ctx'), scatter_dimension=0, tiled=True)  79.8 us
    all_gather x1, waiting for transfers between devices, per_device(): lax.all_gather(reduced[3], 'ctx', axis=0, tiled=True)  47.4 us
    all_gather x1, waiting for transfers between devices, per_device(): lax.all_gather(fc1_weight, 'fsdp', axis=0, tiled=True)  42.7 us
    all_gather x1, waiting for transfers between devices, per_device(): lax.all_gather(qkv_weight, 'fsdp', axis=0, tiled=True)  34.9 us
    all_gather x1, waiting for transfers between devices, per_device(): lax.all_gather(fc2_weight, 'fsdp', axis=0, tiled=True)  32.9 us
  transfers between devices with their start and end apart: 17, of which 15 were waited for; matrix products, arithmetic and copies ran while one was open for 14% of the time, Pallas kernels for 0%

profile of v1, /device:TPU:0, one launch (start us, length us, event | category | flops | bytes accessed | tf_op | source)
XLA Modules:
  0.0 1161.2 jit_solution(14644385917188030824)
XLA Ops:
  24.5 34.9 %all-gather.18.cloned.1.call-done = bf16[2048,3,512]{0,2,1:T(8,128)(2,1)} async-done(((bf16[512,3,512]{0,2,1:T(8,128)(2,1)}), bf16[2048,3,512]{0,2,1:T(8,128)(2,1)}) %all-gather.18.cloned.1.call-update) | async-done | bytes 6291472 | tf_op jit(solution)/shard_map/all_gather | solution.py:96
  69.2 14.3 %all-gather.22.cloned.1.call-done = bf16[2048,512]{1,0:T(8,128)(2,1)} async-done(((bf16[512,512]{1,0:T(8,128)(2,1)}), bf16[2048,512]{1,0:T(8,128)(2,1)}) %all-gather.22.cloned.1.call-update) | async-done | bytes 2097168 | tf_op jit(solution)/shard_map/all_gather | solution.py:97
  90.9 16.0 %all-gather.20.cloned.1.call-done = bf16[1024,2,256]{0,2,1:T(8,128)(2,1)} async-done(((bf16[512,2,256]{0,2,1:T(8,128)(2,1)}), bf16[1024,2,256]{0,2,1:T(8,128)(2,1)}) %all-gather.20.cloned.1.call-update) | async-done | bytes 1048592 | tf_op jit(solution)/shard_map/all_gather | solution.py:144
  114.5 15.7 %all-gather.34.cloned.1.call-done = bf16[1024,1,2,256]{0,3,2,1:T(8,128)(2,1)} async-done(((bf16[512,1,2,256]{0,3,2,1:T(8,128)(2,1)}), bf16[1024,1,2,256]{0,3,2,1:T(8,128)(2,1)}) %all-gather.34.cloned.1.call-update) | async-done | bytes 1048592 | tf_op jit(solution)/shard_map/all_gather | solution.py:145
  152.3 12.5 %reduce-scatter.9.cloned.1.call-done = f32[512,2,256]{2,0,1:T(8,128)} async-done(((f32[1024,2,256]{2,0,1:T(8,128)}), f32[512,2,256]{2,0,1:T(8,128)}) %reduce-scatter.9.cloned.1.call-update) | async-done | bytes 1048592 | tf_op jit(solution)/shard_map/reduce_scatter | solution.py:227
  171.0 28.4 %reduce-scatter.7.cloned.1.call-done = f32[512,2,256]{0,2,1:T(8,128)} async-done(((f32[1024,2,256]{0,2,1:T(8,128)}), f32[512,2,256]{0,2,1:T(8,128)}) %reduce-scatter.7.cloned.1.call-update) | async-done | bytes 1048592 | tf_op jit(solution)/shard_map/reduce_scatter | solution.py:226
  207.1 8.8 fusion.43
  216.7 42.7 %all-gather.24.cloned.1.call-done = bf16[2048,2048]{1,0:T(8,128)(2,1)} async-done(((bf16[512,2048]{1,0:T(8,128)(2,1)}), bf16[2048,2048]{1,0:T(8,128)(2,1)}) %all-gather.24.cloned.1.call-update) | async-done | bytes 8388624 | tf_op jit(solution)/shard_map/all_gather | solution.py:98
  259.3 17.0 %fusion.20 = (bf16[512,2048]{1,0:T(8,128)(2,1)S(1)}, f32[512,2048]{1,0:T(8,128)}) fusion(f32[2048]{0:T(1024)S(1)} %convert_element_type.135, bf16[2048,2048]{1,0:T(8,128)(2,1)} %all-gather.24.cloned.1.call-done, bf16[1,512,2048]{2,1,0:T(8,128)(2,1)S(1)} %copy-done, f32[2048]{0:T(1024)S(1)} %bitcast.223, f32[2048]{0:T(1024)S(1)} %bitcast.214, ...), kind=kOutput, calls=%fused_computation.31 | convolution fusion | flops 4370464768 | bytes 16805888 | tf_op jit(solution)/shard_map/dot_general | solution.py:177
  277.6 8.2 convolution_bitcast_fusion
  286.3 32.9 %all-gather.26.cloned.1.call-done = bf16[2048,2048]{1,0:T(8,128)(2,1)} async-done(((bf16[512,2048]{1,0:T(8,128)(2,1)}), bf16[2048,2048]{1,0:T(8,128)(2,1)}) %all-gather.26.cloned.1.call-update) | async-done | bytes 8388624 | tf_op jit(solution)/shard_map/all_gather | solution.py:99
  319.2 9.4 convert_reduce_fusion.2
  329.9 8.8 fusion.95
  340.3 10.7 fusion.102
  351.0 9.5 fusion.103
  360.6 13.7 %reduce-scatter.13.cloned.1.call-done = f32[256,512]{0,1:T(8,128)} async-done(((f32[2048,512]{0,1:T(8,128)}), f32[256,512]{0,1:T(8,128)}) %reduce-scatter.13.cloned.1.call-update) | async-done | bytes 524304 | tf_op jit(solution)/shard_map/reduce_scatter | solution.py:253
  381.0 8.7 bitcast_add_fusion
  389.8 79.8 %reduce-scatter.11.cloned.1.call-done = f32[256,3,512]{2,0,1:T(8,128)} async-done(((f32[2048,3,512]{2,0,1:T(8,128)}), f32[256,3,512]{2,0,1:T(8,128)}) %reduce-scatter.11.cloned.1.call-update) | async-done | bytes 1572880 | tf_op jit(solution)/shard_map/reduce_scatter | solution.py:252
  469.7 119.5 %reduce-scatter.17.cloned.1.call-done = f32[256,2048]{0,1:T(8,128)} async-done(((f32[2048,2048]{0,1:T(8,128)}), f32[256,2048]{0,1:T(8,128)}) %reduce-scatter.17.cloned.1.call-update) | async-done | bytes 2097168 | tf_op jit(solution)/shard_map/reduce_scatter | solution.py:255
  589.3 119.6 %reduce-scatter.15.cloned.1.call-done = f32[256,2048]{1,0:T(8,128)} async-done(((f32[2048,2048]{1,0:T(8,128)}), f32[256,2048]{1,0:T(8,128)}) %reduce-scatter.15.cloned.1.call-update) | async-done | bytes 2097168 | tf_op jit(solution)/shard_map/reduce_scatter | solution.py:254
  723.3 19.7 %all-gather.30.cloned.1.call-done = f32[512,512]{0,1:T(8,128)} async-done(((f32[256,512]{0,1:T(8,128)}), f32[512,512]{0,1:T(8,128)}) %all-gather.30.cloned.1.call-update) | async-done | bytes 1048592 | tf_op jit(solution)/shard_map/all_gather | solution.py:262
  745.6 291.4 %all-reduce.7.cloned.1.call-done = (f32[512,2048]{1,0:T(8,128)}, f32[512,2048]{1,0:T(8,128)}) async-done(((f32[512,2048]{1,0:T(8,128)}, f32[512,2048]{1,0:T(8,128)}), (f32[512,2048]{1,0:T(8,128)}, f32[512,2048]{1,0:T(8,128)})) %all-reduce.7.cloned.1.call-update) | async-done | bytes 8388624 | tf_op jit(solution)/shard_map/psum | solution.py:184
  1047.2 28.5 %all-reduce.3 = (f32[2048]{0:T(1024)S(1)}, f32[2048]{0:T(1024)S(1)}, f32[3,512]{1,0:T(4,128)}, f32[2048]{0:T(1024)S(1)}, f32[2048]{0:T(1024)}) all-reduce(f32[2048]{0:T(1024)S(1)} %get-tuple-element.60, f32[2048]{0:T(1024)S(1)} %get-tuple-element.63, ...), channel_id=5, replica_groups=mesh['fsdp'=4,'ctx'=2,'tp'=4] {'fsdp','ctx'}, use_global_device_ids=true, to_apply=%region_21.22.clone | all-reduce | flops 9728 | bytes 77824
  1095.5 47.4 %all-gather.32.cloned.1.call-done = f32[512,2048]{0,1:T(8,128)} async-done(((f32[256,2048]{0,1:T(8,128)}), f32[512,2048]{0,1:T(8,128)}) %all-gather.32.cloned.1.call-update) | async-done | bytes 4194320 | tf_op jit(solution)/shard_map/all_gather | solution.py:264
  (216 shorter events, 147.5 us)
Async XLA Ops:
  7.2 52.1 %all-gather.18.cloned.1.call-start = ((), (), s32[]{:S(2)}) async-start(), calls=%async_computation.6 | async-start | bytes 7864320 | tf_op jit(solution)/shard_map/all_gather | solution.py:96
  10.0 73.5 %all-gather.22.cloned.1.call-start = ((), (), s32[]{:S(2)}) async-start(), calls=%async_computation.8 | async-start | bytes 2621440 | tf_op jit(solution)/shard_map/all_gather | solution.py:97
  10.8 96.1 %all-gather.20.cloned.1.call-start = ((), (), s32[]{:S(2)}) async-start(), calls=%async_computation.7 | async-start | bytes 1572864 | tf_op jit(solution)/shard_map/all_gather | solution.py:144
  17.2 48.0 %copy-start.28 = (f32[4,1,512]{2,1,0:T(1,128)}, f32[4,1,512]{2,1,0:T(1,128)S(1)}, u32[]{:S(2)}) copy-start(f32[4,1,512]{2,1,0:T(1,128)S(1)} %convert_element_type.153) | copy-start | bytes 24580
  23.0 45.6 %copy-start.27 = (s32[512]{0:T(512)}, s32[512]{0:T(512)S(1)}, u32[]{:S(2)}) copy-start(s32[512]{0:T(512)S(1)} %get-tuple-element.65) | copy-start | bytes 6148
  24.5 41.1 %copy-start.21 = (f32[512,32]{0,1:T(8,128)}, f32[512,32]{0,1:T(8,128)S(1)}, u32[]{:S(2)}) copy-start(f32[512,32]{0,1:T(8,128)S(1)} %get-tuple-element.92) | copy-start | bytes 196612
  67.8 62.4 %all-gather.34.cloned.1.call-start = ((), (), s32[]{:S(2)}) async-start(), calls=%async_computation.20 | async-start | bytes 1572864 | tf_op jit(solution)/shard_map/all_gather | solution.py:145
  90.0 74.9 %reduce-scatter.9.cloned.1.call-start = ((), (), s32[]{:S(2)}) async-start(), calls=%async_computation.12 | async-start | bytes 3145728 | tf_op jit(solution)/shard_map/reduce_scatter | solution.py:227
  114.3 85.2 %reduce-scatter.7.cloned.1.call-start = ((), (), s32[]{:S(2)}) async-start(), calls=%async_computation.11 | async-start | bytes 3145728 | tf_op jit(solution)/shard_map/reduce_scatter | solution.py:226
  138.6 120.8 %all-gather.24.cloned.1.call-start = ((), (), s32[]{:S(2)}) async-start(), calls=%async_computation.9 | async-start | bytes 10485760 | tf_op jit(solution)/shard_map/all_gather | solution.py:98
  139.3 179.9 %all-gather.26.cloned.1.call-start = ((), (), s32[]{:S(2)}) async-start(), calls=%async_computation.10 | async-start | bytes 10485760 | tf_op jit(solution)/shard_map/all_gather | solution.py:99
  140.1 234.2 %reduce-scatter.13.cloned.1.call-start = ((), (), s32[]{:S(2)}) async-start(), calls=%async_computation.15 | async-start | bytes 4718592 | tf_op jit(solution)/shard_map/reduce_scatter | solution.py:253
  147.5 322.2 %reduce-scatter.11.cloned.1.call-start = ((), (), s32[]{:S(2)}) async-start(), calls=%async_computation.13 | async-start | bytes 14155776 | tf_op jit(solution)/shard_map/reduce_scatter | solution.py:252
  216.0 43.3 %copy-start.29 = (f32[4,1,512]{2,1,0:T(1,128)S(1)}, f32[4,1,512]{2,1,0:T(1,128)}, u32[]{:S(2)}) copy-start(f32[4,1,512]{2,1,0:T(1,128)} %copy-done.28) | copy-start | bytes 24580
  216.0 373.2 %reduce-scatter.17.cloned.1.call-start = ((), (), s32[]{:S(2)}) async-start(), calls=%async_computation.18 | async-start | bytes 18874368 | tf_op jit(solution)/shard_map/reduce_scatter | solution.py:255
  285.8 423.1 %reduce-scatter.15.cloned.1.call-start = ((), (), s32[]{:S(2)}) async-start(), calls=%async_computation.17 | async-start | bytes 18874368 | tf_op jit(solution)/shard_map/reduce_scatter | solution.py:254
  338.8 404.3 %all-gather.30.cloned.1.call-start = ((), (), s32[]{:S(2)}) async-start(), calls=%async_computation.16 | async-start | bytes 1572864 | tf_op jit(solution)/shard_map/all_gather | solution.py:262
  374.3 662.7 %all-reduce.7.cloned.1.call-start = ((), (), s32[]{:S(2)}) async-start(), calls=%async_computation.21 | async-start | bytes 16777216 | tf_op jit(solution)/shard_map/psum | solution.py:184
  389.7 320.6 %copy-start.35 = (bf16[512]{0:T(512)(128)(2,1)S(1)}, bf16[512]{0:T(512)(128)(2,1)}, u32[]{:S(2)}) copy-start(bf16[512]{0:T(512)(128)(2,1)} %param.22) | copy-start | bytes 3076
  389.7 320.7 %copy-start.36 = (bf16[512]{0:T(512)(128)(2,1)S(1)}, bf16[512]{0:T(512)(128)(2,1)}, u32[]{:S(2)}) copy-start(bf16[512]{0:T(512)(128)(2,1)} %param.26) | copy-start | bytes 3076
  389.7 320.7 %copy-start.39 = (u32[32]{0:T(128)S(1)}, u32[32]{0:T(128)}, u32[]{:S(2)}) copy-start(u32[32]{0:T(128)} %constant.181) | copy-start | bytes 388
  389.8 699.0 %all-gather.28.cloned.1.call-start = ((), (), s32[]{:S(2)}) async-start(), calls=%async_computation.14 | async-start | bytes 4718592 | tf_op jit(solution)/shard_map/all_gather | solution.py:261
  469.7 673.3 %all-gather.32.cloned.1.call-start = ((), (), s32[]{:S(2)}) async-start(), calls=%async_computation.19 | async-start | bytes 6291456 | tf_op jit(solution)/shard_map/all_gather | solution.py:264
  708.9 379.9 %collective-permute-start = (f32[256,2048]{1,0:T(8,128)}, f32[256,2048]{1,0:T(8,128)}, u32[]{:S(2)}, u32[]{:S(2)}) collective-permute-start(f32[256,2048]{1,0:T(8,128)} %reduce-scatter.15.cloned.1.call-done), channel_id=1, source_target_pairs={{0,4},{4,0},{1,5},{5,1},{2,6},{6,2},{3,7},{7,3},{8,12},{12,8},{9,1... | collective-permute-start | bytes 6291464 | tf_op jit(solution)/shard_map/ppermute | solution.py:18
  (37 other events, 229.5 us)
Sparse Core Ops, SparseCore 0:
  10.2 49.1 all-gather.17
  60.9 22.5 all-gather.21
  85.6 21.2 all-gather.19
  108.9 21.2 all-gather.33
  132.9 31.9 reduce-scatter.8
  167.5 31.8 reduce-scatter.6
  201.0 58.2 all-gather.23
  260.9 58.2 all-gather.25
  323.1 51.0 reduce-scatter.12
  377.6 92.0 reduce-scatter.10
  473.2 115.9 reduce-scatter.16
  592.7 116.1 reduce-scatter.14
  710.4 32.6 all-gather.29
  746.1 290.8 all-reduce.6
  1038.4 46.3 all-gather.27
  1086.2 56.7 all-gather.31
